TPU v7x, 32 devices: a whole 2x2x4 slice. The times are simulated.
32 devices in a mesh: row: 8 (over z, y), col: 4 (over x, core).
Axes of the slice: x: 2, y: 2, z: 4, core: 2. Of those that a mesh axis runs over, the one named last changes fastest.
Arguments:
- front: bfloat16 [8192, 8192], P('row', 'col'), may hold values from -0.125 to 0.125
- tile_mask: int32 [32, 32], P('row', 'col'), may hold values 0 or 1
- probes: bfloat16 [8192, 256], P(('col', 'row')), may hold values from -6 to 6
- coupling: float32 [8192, 256], P(('row', 'col')), may hold values from -0.375 to 0.375
Outputs:
- leaf_basis: float32 [8192, 256], P(('row', 'col'))
- upper_transfer: float32 [4, 8192, 256], P(None, ('row', 'col'))
Inputs may be any that keep to these rules, and one draw needn't show every extreme that they name: `tile_mask`: 1 where a tile of the front is present, 0 where it is absent.
All inputs are finite; a program needn't handle non-finite values. No bound on the sum of `tile_mask` on one device may be relied on, other than what follows from the above.
Results may differ from a plain program's by a relative error of at most 0.0003.
Values may be sent and summed in bfloat16 or wider, within the bound.
No kernel may reach another device: no remote copies, remote signals or barrier semaphores. Data moves between devices by JAX's collectives and lax.ppermute only.
A program may use at most 128 MiB of HBM per device.

v0:
```python
import jax
import jax.numpy as jnp
from jax import lax
from jax.sharding import PartitionSpec as P


def from_root(x, axis, root):
    mine = lax.axis_index(axis) == root
    return lax.psum(jnp.where(mine, x, jnp.zeros_like(x)), axis)


def from_partner(value, axis, distance):
    mask = 2**distance
    pairs = [(source, source ^ mask) for source in range(lax.axis_size(axis))]
    return lax.ppermute(value, axis, pairs)


def matmul_high(left, right):
    return jnp.matmul(left, right, precision=lax.Precision.HIGHEST)


def transpose_last(array):
    return jnp.swapaxes(array, -1, -2)


def merge_pair(top_node, bottom_node, level_index):
    top_s, top_w, top_p = top_node
    bottom_s, bottom_w, bottom_p = bottom_node
    if level_index > 1:
        factor = 2.0 ** (-(level_index - 1) / 2.0)
        top_s = top_s - factor * matmul_high(top_p, bottom_w)
        bottom_s = bottom_s - factor * matmul_high(bottom_p, top_w)
    stacked = jnp.concatenate([top_s, bottom_s], axis=-2)
    gram_matrix = matmul_high(transpose_last(stacked), stacked)
    probe_count = gram_matrix.shape[-1]
    shift_value = 0.001 * (jnp.trace(gram_matrix, axis1=-2, axis2=-1) / probe_count + 1e-06)
    gram_matrix = gram_matrix + shift_value[..., None, None] * jnp.eye(
        probe_count, dtype=jnp.float32
    )
    lower_factor = jnp.linalg.cholesky(gram_matrix)
    basis_rows = jax.scipy.linalg.solve_triangular(
        lower_factor, transpose_last(stacked), lower=True
    )
    new_w = matmul_high(basis_rows, jnp.concatenate([top_w, bottom_w], axis=-2))
    row_total = top_s.shape[-2]
    top_half = transpose_last(basis_rows[..., :row_total])
    bottom_half = transpose_last(basis_rows[..., row_total:])
    return ((transpose_last(lower_factor), new_w, top_p + bottom_p), top_half, bottom_half)


def pair_step(node_state, partner, side_bit, level_index):
    is_top = side_bit == 0
    top_node = tuple((jnp.where(is_top, mine, other) for mine, other in zip(node_state, partner)))
    bottom_node = tuple(
        (jnp.where(is_top, other, mine) for mine, other in zip(node_state, partner))
    )
    parent, top_half, bottom_half = merge_pair(top_node, bottom_node, level_index)
    return (parent, jnp.where(is_top, top_half, bottom_half))


def pack_state(node_state):
    return jnp.concatenate(node_state, axis=0)


def unpack_state(packed, sample_rows, probe_rows):
    return (
        packed[:sample_rows],
        packed[sample_rows : sample_rows + probe_rows],
        packed[sample_rows + probe_rows :],
    )


def shards(front, tile_mask, probes, coupling):
    col_count = lax.axis_size("col")
    row_count = lax.axis_size("row")
    row_index = lax.axis_index("row")
    col_index = lax.axis_index("col")
    leaf_rows = front.shape[0] // col_count
    probe_count = probes.shape[1]
    col_levels = col_count.bit_length() - 1
    row_levels = row_count.bit_length() - 1
    probe_block = lax.all_gather(probes, "row", axis=0, tiled=True)
    tile_above = row_index * col_count + jnp.arange(col_count, dtype=jnp.int32)
    tile_across = col_index * row_count + jnp.arange(row_count, dtype=jnp.int32)
    keep_tiles = tile_mask * (tile_above[:, None] // 2 != tile_across[None, :] // 2).astype(
        jnp.int32
    )
    masked = (
        front.reshape(col_count, leaf_rows, row_count, leaf_rows)
        * keep_tiles.astype(jnp.bfloat16)[:, None, :, None]
    )
    partial_value = jnp.dot(
        masked.reshape(front.shape), probe_block, preferred_element_type=jnp.float32
    )
    sample = lax.psum_scatter(partial_value, "col", scatter_dimension=0, tiled=True)
    offset = row_index * col_count % row_count * leaf_rows
    root_col = row_index * col_count // row_count
    offered = lax.dynamic_slice_in_dim(probe_block, offset, col_count * leaf_rows, 0)
    group_probes = from_root(offered, "col", root_col)
    own_probe = lax.dynamic_slice_in_dim(group_probes, col_index * leaf_rows, leaf_rows, 0).astype(
        jnp.float32
    )
    halves = []
    node_state = (sample, own_probe, coupling)
    for bit_index in range(col_levels):
        sample_rows = node_state[0].shape[0]
        probe_rows = node_state[1].shape[0]
        packed = from_partner(pack_state(node_state), "col", bit_index)
        partner = unpack_state(packed, sample_rows, probe_rows)
        node_state, own_half = pair_step(
            node_state, partner, col_index >> bit_index & 1, bit_index + 1
        )
        halves.append(own_half)
    for bit_index in range(row_levels):
        packed = from_partner(pack_state(node_state), "row", bit_index)
        partner = unpack_state(packed, probe_count, probe_count)
        node_state, own_half = pair_step(
            node_state, partner, row_index >> bit_index & 1, col_levels + bit_index + 1
        )
        halves.append(own_half)
    return (halves[0], jnp.stack(halves[1:], axis=0))


def solution(mesh):
    in_specs = (P("row", "col"), P("row", "col"), P(("col", "row"), None), P(("row", "col"), None))
    out_specs = (P(("row", "col"), None), P(None, ("row", "col"), None))
    return jax.shard_map(shards, mesh=mesh, in_specs=in_specs, out_specs=out_specs, check_vma=False)
```

profile of v0, /device:TPU:0, one launch (start us, length us, event | category | flops | bytes accessed | tf_op | source)
XLA Modules:
  0.0 565.7 jit_solution(5704452580519430025)
XLA Ops:
  13.5 39.2 %all-gather.2.cloned.1.call-done = bf16[2048,256]{0,1:T(8,128)(2,1)} async-done(((bf16[256,256]{0,1:T(8,128)(2,1)}), bf16[2048,256]{0,1:T(8,128)(2,1)}) %all-gather.2.cloned.1.call-update) | async-done | bytes 1048592 | tf_op jit(solution)/shard_map/all_gather | solution.py:82
  61.1 26.4 %all-reduce.3.cloned.1.call-done = bf16[1024,256]{0,1:T(8,128)(2,1)} async-done(((bf16[1024,256]{0,1:T(8,128)(2,1)}), bf16[1024,256]{0,1:T(8,128)(2,1)}) %all-reduce.3.cloned.1.call-update) | async-done | bytes 524304 | tf_op jit(solution)/shard_map/psum | solution.py:9
  88.4 27.1 %reduce-scatter.2.cloned.1.call-done = f32[256,256]{0,1:T(8,128)} async-done(((f32[1024,256]{0,1:T(8,128)}), f32[256,256]{0,1:T(8,128)}) %reduce-scatter.2.cloned.1.call-update) | async-done | bytes 262160 | tf_op jit(solution)/shard_map/reduce_scatter | solution.py:95
  122.1 11.7 %cholesky.256 = f32[128,128]{1,0:T(8,128)S(1)} custom-call(f32[128,128]{1,0:T(8,128)S(1)} %cholesky.422), custom_call_target="Cholesky" | custom-call | tf_op jit(solution)/shard_map/jit(cholesky)/cholesky | solution.py:40
  144.5 12.1 %cholesky.273 = f32[128,128]{1,0:T(8,128)S(1)} custom-call(f32[128,128]{1,0:T(8,128)S(1)} %convolution_subtract_fusion.9), custom_call_target="Cholesky" | custom-call | tf_op jit(solution)/shard_map/jit(cholesky)/cholesky | solution.py:40
  162.9 19.7 %custom-call.20 = f32[2,128,128]{1,2,0:T(8,128)S(1)} custom-call(f32[2,128,128]{2,1,0:T(8,128)S(1)} %get-tuple-element.36), custom_call_target="InvertDiagBlocksLowerTriangular" | custom-call | tf_op jit(solution)/shard_map/jit(_solve_triangular)/triangular_solve | solution.py:41
  185.3 19.2 %collective-permute-done.1 = f32[768,256]{0,1:T(8,128)S(1)} collective-permute-done((f32[768,256]{0,1:T(8,128)S(1)}, f32[768,256]{0,1:T(8,128)S(1)}, u32[]{:S(2)}, u32[]{:S(2)}) %collective-permute-start.1) | collective-permute-done | bytes 786464 | tf_op jit(solution)/shard_map/ppermute | solution.py:15
  207.6 11.7 %cholesky.290 = f32[128,128]{1,0:T(8,128)S(1)} custom-call(f32[128,128]{1,0:T(8,128)S(1)} %cholesky.425), custom_call_target="Cholesky" | custom-call | tf_op jit(solution)/shard_map/jit(cholesky)/cholesky | solution.py:40
  219.4 9.8 %custom-call.21 = f32[1,128,128]{1,2,0:T(8,128)S(1)} custom-call(f32[1,128,128]{2,1,0:T(8,128)S(1)} %get-tuple-element.130), custom_call_target="InvertDiagBlocksLowerTriangular" | custom-call | tf_op jit(solution)/shard_map/jit(cholesky)/cholesky | solution.py:40
  229.9 11.9 %cholesky.307 = f32[128,128]{1,0:T(8,128)S(1)} custom-call(f32[128,128]{1,0:T(8,128)S(1)} %convolution_subtract_fusion.8), custom_call_target="Cholesky" | custom-call | tf_op jit(solution)/shard_map/jit(cholesky)/cholesky | solution.py:40
  248.5 19.7 %custom-call.22 = f32[2,128,128]{1,2,0:T(8,128)S(1)} custom-call(f32[2,128,128]{2,1,0:T(8,128)S(1)} %get-tuple-element.37), custom_call_target="InvertDiagBlocksLowerTriangular" | custom-call | tf_op jit(solution)/shard_map/jit(_solve_triangular)/triangular_solve | solution.py:41
  271.9 17.4 %collective-permute-done.2 = f32[768,256]{0,1:T(8,128)} collective-permute-done((f32[768,256]{0,1:T(8,128)S(1)}, f32[768,256]{0,1:T(8,128)}, u32[]{:S(2)}, u32[]{:S(2)}) %collective-permute-start.2) | collective-permute-done | bytes 786464 | tf_op jit(solution)/shard_map/ppermute | solution.py:15
  295.5 11.7 %cholesky.324 = f32[128,128]{1,0:T(8,128)S(1)} custom-call(f32[128,128]{1,0:T(8,128)S(1)} %cholesky.428), custom_call_target="Cholesky" | custom-call | tf_op jit(solution)/shard_map/jit(cholesky)/cholesky | solution.py:40
  307.2 9.8 %custom-call.23 = f32[1,128,128]{1,2,0:T(8,128)S(1)} custom-call(f32[1,128,128]{2,1,0:T(8,128)S(1)} %get-tuple-element.126), custom_call_target="InvertDiagBlocksLowerTriangular" | custom-call | tf_op jit(solution)/shard_map/jit(cholesky)/cholesky | solution.py:40
  317.7 12.1 %cholesky.341 = f32[128,128]{1,0:T(8,128)S(1)} custom-call(f32[128,128]{1,0:T(8,128)S(1)} %convolution_subtract_fusion.7), custom_call_target="Cholesky" | custom-call | tf_op jit(solution)/shard_map/jit(cholesky)/cholesky | solution.py:40
  336.5 19.7 %custom-call.24 = f32[2,128,128]{1,2,0:T(8,128)S(1)} custom-call(f32[2,128,128]{2,1,0:T(8,128)S(1)} %get-tuple-element.38), custom_call_target="InvertDiagBlocksLowerTriangular" | custom-call | tf_op jit(solution)/shard_map/jit(_solve_triangular)/triangular_solve | solution.py:41
  360.0 16.5 %collective-permute-done.3 = f32[768,256]{0,1:T(8,128)} collective-permute-done((f32[768,256]{0,1:T(8,128)S(1)}, f32[768,256]{0,1:T(8,128)}, u32[]{:S(2)}, u32[]{:S(2)}) %collective-permute-start.3) | collective-permute-done | bytes 786464 | tf_op jit(solution)/shard_map/ppermute | solution.py:15
  384.3 11.7 %cholesky.358 = f32[128,128]{1,0:T(8,128)S(1)} custom-call(f32[128,128]{1,0:T(8,128)S(1)} %cholesky.431), custom_call_target="Cholesky" | custom-call | tf_op jit(solution)/shard_map/jit(cholesky)/cholesky | solution.py:40
  408.3 11.9 %cholesky.375 = f32[128,128]{1,0:T(8,128)S(1)} custom-call(f32[128,128]{1,0:T(8,128)S(1)} %convolution_subtract_fusion.6), custom_call_target="Cholesky" | custom-call | tf_op jit(solution)/shard_map/jit(cholesky)/cholesky | solution.py:40
  429.3 20.5 %custom-call.26 = f32[2,128,128]{1,2,0:T(8,128)S(1)} custom-call(f32[2,128,128]{2,1,0:T(8,128)} %copy-done.7), custom_call_target="InvertDiagBlocksLowerTriangular" | custom-call | tf_op jit(solution)/shard_map/jit(_solve_triangular)/triangular_solve | solution.py:41
  460.7 29.8 %collective-permute-done.4 = f32[768,256]{0,1:T(8,128)} collective-permute-done((f32[768,256]{0,1:T(8,128)}, f32[768,256]{0,1:T(8,128)}, u32[]{:S(2)}, u32[]{:S(2)}) %collective-permute-start.4) | collective-permute-done | bytes 786464 | tf_op jit(solution)/shard_map/ppermute | solution.py:15
  495.8 11.7 %cholesky.392 = f32[128,128]{1,0:T(8,128)S(1)} custom-call(f32[128,128]{1,0:T(8,128)S(1)} %cholesky.434), custom_call_target="Cholesky" | custom-call | tf_op jit(solution)/shard_map/jit(cholesky)/cholesky | solution.py:40
  517.9 11.9 %cholesky.409 = f32[128,128]{1,0:T(8,128)S(1)} custom-call(f32[128,128]{1,0:T(8,128)S(1)} %convolution_subtract_fusion.5), custom_call_target="Cholesky" | custom-call | tf_op jit(solution)/shard_map/jit(cholesky)/cholesky | solution.py:40
  536.7 19.7 %custom-call.28 = f32[2,128,128]{1,2,0:T(8,128)S(1)} custom-call(f32[2,128,128]{2,1,0:T(8,128)S(1)} %get-tuple-element.40), custom_call_target="InvertDiagBlocksLowerTriangular" | custom-call | tf_op jit(solution)/shard_map/jit(_solve_triangular)/triangular_solve | solution.py:41
  (207 shorter events, 148.0 us)
Async XLA Ops:
  7.2 45.6 %all-gather.2.cloned.1.call-start = ((), (), s32[]{:S(2)}) async-start(), calls=%async_computation.1 | async-start | bytes 1179648 | tf_op jit(solution)/shard_map/all_gather | solution.py:82
  8.9 78.6 %all-reduce.3.cloned.1.call-start = ((), (), s32[]{:S(2)}) async-start(), calls=%async_computation.3 | async-start | bytes 1048576 | tf_op jit(solution)/shard_map/psum | solution.py:9
  54.7 60.8 %reduce-scatter.2.cloned.1.call-start = ((), (), s32[]{:S(2)}) async-start(), calls=%async_computation.2 | async-start | bytes 1310720 | tf_op jit(solution)/shard_map/reduce_scatter | solution.py:95
  55.0 6.0 %copy-start.6 = (f32[256,256]{1,0:T(8,128)S(1)}, f32[256,256]{1,0:T(8,128)}, u32[]{:S(2)}) copy-start(f32[256,256]{1,0:T(8,128)} %param.10) | copy-start | bytes 786436
  116.5 2.4 collective-permute-start
  184.8 19.7 %collective-permute-start.1 = (f32[768,256]{0,1:T(8,128)S(1)}, f32[768,256]{0,1:T(8,128)S(1)}, u32[]{:S(2)}, u32[]{:S(2)}) collective-permute-start(f32[768,256]{0,1:T(8,128)S(1)} %pad_maximum_fusion.2), channel_id=1, source_target_pairs={{0,2},{1,3},{2,0},{3,1},{4,6},{5,7},{6,4},{7,5},{8,10},{9,11},{10,... | collective-permute-start | bytes 2359304 | tf_op jit(solution)/shard_map/ppermute | solution.py:15
  270.4 18.9 %collective-permute-start.2 = (f32[768,256]{0,1:T(8,128)S(1)}, f32[768,256]{0,1:T(8,128)}, u32[]{:S(2)}, u32[]{:S(2)}) collective-permute-start(f32[768,256]{0,1:T(8,128)S(1)} %pad_maximum_fusion.3), channel_id=1, source_target_pairs={{0,4},{4,0},{8,12},{12,8},{16,20},{20,16},{24,28},{28,24},{1,5},{5... | collective-permute-start | bytes 2359304 | tf_op jit(solution)/shard_map/ppermute | solution.py:15
  358.5 18.0 %collective-permute-start.3 = (f32[768,256]{0,1:T(8,128)S(1)}, f32[768,256]{0,1:T(8,128)}, u32[]{:S(2)}, u32[]{:S(2)}) collective-permute-start(f32[768,256]{0,1:T(8,128)S(1)} %pad_maximum_fusion.4), channel_id=1, source_target_pairs={{0,8},{4,12},{8,0},{12,4},{16,24},{20,28},{24,16},{28,20},{1,9},{5... | collective-permute-start | bytes 2359304 | tf_op jit(solution)/shard_map/ppermute | solution.py:15
  384.3 11.8 %copy-start.5 = (f32[256,256]{1,0:T(8,128)}, f32[256,256]{1,0:T(8,128)S(1)}, u32[]{:S(2)}) copy-start(f32[256,256]{1,0:T(8,128)S(1)} %fusion.58) | copy-start | bytes 786436
  420.2 2.7 copy-start.1
  427.9 0.7 copy-start.7
  428.6 0.7 copy-start
  455.4 35.1 %collective-permute-start.4 = (f32[768,256]{0,1:T(8,128)}, f32[768,256]{0,1:T(8,128)}, u32[]{:S(2)}, u32[]{:S(2)}) collective-permute-start(f32[768,256]{0,1:T(8,128)} %pad_maximum_fusion.5), channel_id=1, source_target_pairs={{0,16},{4,20},{8,24},{12,28},{16,0},{20,4},{24,8},{28,12},{1,17},{... | collective-permute-start | bytes 2359304 | tf_op jit(solution)/shard_map/ppermute | solution.py:15
  494.8 63.1 %copy-start.2 = (f32[1,256,256]{2,1,0:T(8,128)S(1)}, f32[1,256,256]{2,1,0:T(8,128)}, u32[]{:S(2)}) copy-start(f32[1,256,256]{2,1,0:T(8,128)} %fusion.41) | copy-start | bytes 786436
  494.8 63.1 %copy-start.3 = (f32[1,256,256]{2,1,0:T(8,128)S(1)}, f32[1,256,256]{2,1,0:T(8,128)}, u32[]{:S(2)}) copy-start(f32[1,256,256]{2,1,0:T(8,128)} %fusion.37) | copy-start | bytes 786436
  494.8 63.1 %copy-start.4 = (f32[1,256,256]{2,1,0:T(8,128)S(1)}, f32[1,256,256]{2,1,0:T(8,128)}, u32[]{:S(2)}) copy-start(f32[1,256,256]{2,1,0:T(8,128)} %fusion.33) | copy-start | bytes 786436
Sparse Core Ops, SparseCore 0:
  10.6 42.1 all-gather.1
  55.1 32.3 all-reduce.2
  90.6 24.8 reduce-scatter.1
where the time goes:
time: 569 us; the launch traced here: 566 us
  other arithmetic  289 us (51%)
  waiting for transfers between devices  178 us (31%)
  matrix products  38.1 us (7%)
  local copies, waits for them, and re-layouts  29.5 us (5%)
  between operations  25 us (4%)
  starting transfers between devices  6.23 us (1%)
    another operation x34, other arithmetic, merge_pair(): lower_factor = jnp.linalg.cholesky(gram_matrix)  174 us
    another operation x10, other arithmetic, merge_pair(): jax.scipy.linalg.solve_triangular(lower_factor, transpose_last(stacked),...  100 us
    ppermute x5, waiting for transfers between devices, from_partner(): return lax.ppermute(value, axis, pairs)  85.1 us
    all_gather x1, waiting for transfers between devices, shards(): probe_block = lax.all_gather(probes, 'row', axis=0, tiled=True)  39.2 us
    reduce_scatter x1, waiting for transfers between devices, shards(): lax.psum_scatter(partial_value, 'col', scatter_dimension=0, tiled=True)  27.1 us
    psum x1, waiting for transfers between devices, from_root(): return lax.psum(jnp.where(mine, x, jnp.zeros_like(x)), axis)  26.4 us
    another operation x41, local copies, waits for them, and re-layouts, merge_pair(): jax.scipy.linalg.solve_triangular(lower_factor, transpose_last(stacked),...  20.7 us
    dot_general x17, matrix products, matmul_high(): return jnp.matmul(left, right, precision=lax.Precision.HIGHEST)  18.2 us
  transfers between devices with their start and end apart: 8, of which 8 were waited for; matrix products, arithmetic and copies ran while one was open for 3% of the time, Pallas kernels for 0%

commit v1 on v0

--- a/solution.py
+++ b/solution.py
@@ -79,7 +79,9 @@
     probe_count = probes.shape[1]
     col_levels = col_count.bit_length() - 1
     row_levels = row_count.bit_length() - 1
-    probe_block = lax.all_gather(probes, "row", axis=0, tiled=True)
+    probe_block = jnp.concatenate(
+        lax.all_to_all(jnp.stack([probes] * lax.axis_size("row")), "row", 0, 0), axis=0
+    )
     tile_above = row_index * col_count + jnp.arange(col_count, dtype=jnp.int32)
     tile_across = col_index * row_count + jnp.arange(row_count, dtype=jnp.int32)
     keep_tiles = tile_mask * (tile_above[:, None] // 2 != tile_across[None, :] // 2).astype(

time: 569 us -> 558 us (0.981)
  waiting for transfers between devices: 178 us -> 160 us
  starting transfers between devices: 6.23 us -> 13.5 us
    all_gather x1 -> x0, waiting for transfers between devices: 39.2 us -> none  [shards(): probe_block = lax.all_gather(probes, 'row', axis=0, tiled=True)]
    all_to_all x0 -> x1, waiting for transfers between devices: none -> 21.2 us  [shards(): lax.all_to_all(jnp.stack([probes] * lax.axis_size('row')), 'row', 0, 0)]
    all_to_all x0 -> x1, starting transfers between devices: none -> 7.31 us  [shards(): lax.all_to_all(jnp.stack([probes] * lax.axis_size('row')), 'row', 0, 0)]
where the time goes in v1:
time: 558 us; the launch traced here: 554 us
  other arithmetic  288 us (52%)
  waiting for transfers between devices  160 us (29%)
  matrix products  37.9 us (7%)
  local copies, waits for them, and re-layouts  30 us (5%)
  between operations  25.3 us (5%)
  starting transfers between devices  13.5 us (2%)
    another operation x34, other arithmetic, merge_pair(): lower_factor = jnp.linalg.cholesky(gram_matrix)  174 us
    another operation x10, other arithmetic, merge_pair(): jax.scipy.linalg.solve_triangular(lower_factor, transpose_last(stacked),...  100 us
    ppermute x5, waiting for transfers between devices, from_partner(): return lax.ppermute(value, axis, pairs)  85.1 us
    reduce_scatter x1, waiting for transfers between devices, shards(): lax.psum_scatter(partial_value, 'col', scatter_dimension=0, tiled=True)  27.1 us
    psum x1, waiting for transfers between devices, from_root(): return lax.psum(jnp.where(mine, x, jnp.zeros_like(x)), axis)  26.4 us
    all_to_all x1, waiting for transfers between devices, shards(): lax.all_to_all(jnp.stack([probes] * lax.axis_size('row')), 'row', 0, 0)  21.2 us
    another operation x41, local copies, waits for them, and re-layouts, merge_pair(): jax.scipy.linalg.solve_triangular(lower_factor, transpose_last(stacked),...  20.7 us
    dot_general x17, matrix products, matmul_high(): return jnp.matmul(left, right, precision=lax.Precision.HIGHEST)  18.2 us
  transfers between devices with their start and end apart: 8, of which 8 were waited for; matrix products, arithmetic and copies ran while one was open for 3% of the time, Pallas kernels for 0%

profile of v1, /device:TPU:0, one launch (start us, length us, event | category | flops | bytes accessed | tf_op | source)
XLA Modules:
  0.0 554.5 jit_solution(3363246605068466303)
XLA Ops:
  21.1 21.2 %all-to-all-done = bf16[8,256,256]{1,2,0:T(8,128)(2,1)S(1)} async-done(((bf16[8,256,256]{1,2,0:T(8,128)(2,1)}), bf16[8,256,256]{1,2,0:T(8,128)(2,1)S(1)}, u32[]{:S(2)}, u32[]{:S(2)}) %all-to-all-start) | async-done | bytes 1048608 | tf_op jit(solution)/shard_map/all_to_all | solution.py:83
  49.6 26.4 %all-reduce.3.cloned.1.call-done = bf16[1024,256]{0,1:T(8,128)(2,1)} async-done(((bf16[1024,256]{0,1:T(8,128)(2,1)}), bf16[1024,256]{0,1:T(8,128)(2,1)}) %all-reduce.3.cloned.1.call-update) | async-done | bytes 524304 | tf_op jit(solution)/shard_map/psum | solution.py:9
  76.9 27.1 %reduce-scatter.2.cloned.1.call-done = f32[256,256]{0,1:T(8,128)} async-done(((f32[1024,256]{0,1:T(8,128)}), f32[256,256]{0,1:T(8,128)}) %reduce-scatter.2.cloned.1.call-update) | async-done | bytes 262160 | tf_op jit(solution)/shard_map/reduce_scatter | solution.py:97
  110.6 11.7 %cholesky.256 = f32[128,128]{1,0:T(8,128)S(1)} custom-call(f32[128,128]{1,0:T(8,128)S(1)} %cholesky.422), custom_call_target="Cholesky" | custom-call | tf_op jit(solution)/shard_map/jit(cholesky)/cholesky | solution.py:40
  122.3 9.8 %custom-call.19 = f32[1,128,128]{1,2,0:T(8,128)S(1)} custom-call(f32[1,128,128]{2,1,0:T(8,128)S(1)} %get-tuple-element.134), custom_call_target="InvertDiagBlocksLowerTriangular" | custom-call | tf_op jit(solution)/shard_map/jit(cholesky)/cholesky | solution.py:40
  132.9 12.1 %cholesky.273 = f32[128,128]{1,0:T(8,128)S(1)} custom-call(f32[128,128]{1,0:T(8,128)S(1)} %convolution_subtract_fusion.9), custom_call_target="Cholesky" | custom-call | tf_op jit(solution)/shard_map/jit(cholesky)/cholesky | solution.py:40
  151.4 19.7 %custom-call.20 = f32[2,128,128]{1,2,0:T(8,128)S(1)} custom-call(f32[2,128,128]{2,1,0:T(8,128)S(1)} %get-tuple-element.36), custom_call_target="InvertDiagBlocksLowerTriangular" | custom-call | tf_op jit(solution)/shard_map/jit(_solve_triangular)/triangular_solve | solution.py:41
  173.7 19.2 %collective-permute-done.1 = f32[768,256]{0,1:T(8,128)S(1)} collective-permute-done((f32[768,256]{0,1:T(8,128)S(1)}, f32[768,256]{0,1:T(8,128)S(1)}, u32[]{:S(2)}, u32[]{:S(2)}) %collective-permute-start.1) | collective-permute-done | bytes 786464 | tf_op jit(solution)/shard_map/ppermute | solution.py:15
  196.1 11.7 %cholesky.290 = f32[128,128]{1,0:T(8,128)S(1)} custom-call(f32[128,128]{1,0:T(8,128)S(1)} %cholesky.425), custom_call_target="Cholesky" | custom-call | tf_op jit(solution)/shard_map/jit(cholesky)/cholesky | solution.py:40
  207.8 9.8 %custom-call.21 = f32[1,128,128]{1,2,0:T(8,128)S(1)} custom-call(f32[1,128,128]{2,1,0:T(8,128)S(1)} %get-tuple-element.130), custom_call_target="InvertDiagBlocksLowerTriangular" | custom-call | tf_op jit(solution)/shard_map/jit(cholesky)/cholesky | solution.py:40
  218.3 11.9 %cholesky.307 = f32[128,128]{1,0:T(8,128)S(1)} custom-call(f32[128,128]{1,0:T(8,128)S(1)} %convolution_subtract_fusion.8), custom_call_target="Cholesky" | custom-call | tf_op jit(solution)/shard_map/jit(cholesky)/cholesky | solution.py:40
  236.9 19.7 %custom-call.22 = f32[2,128,128]{1,2,0:T(8,128)S(1)} custom-call(f32[2,128,128]{2,1,0:T(8,128)S(1)} %get-tuple-element.37), custom_call_target="InvertDiagBlocksLowerTriangular" | custom-call | tf_op jit(solution)/shard_map/jit(_solve_triangular)/triangular_solve | solution.py:41
  260.4 17.4 %collective-permute-done.2 = f32[768,256]{0,1:T(8,128)} collective-permute-done((f32[768,256]{0,1:T(8,128)S(1)}, f32[768,256]{0,1:T(8,128)}, u32[]{:S(2)}, u32[]{:S(2)}) %collective-permute-start.2) | collective-permute-done | bytes 786464 | tf_op jit(solution)/shard_map/ppermute | solution.py:15
  283.9 11.7 %cholesky.324 = f32[128,128]{1,0:T(8,128)S(1)} custom-call(f32[128,128]{1,0:T(8,128)S(1)} %cholesky.428), custom_call_target="Cholesky" | custom-call | tf_op jit(solution)/shard_map/jit(cholesky)/cholesky | solution.py:40
  306.2 12.1 %cholesky.341 = f32[128,128]{1,0:T(8,128)S(1)} custom-call(f32[128,128]{1,0:T(8,128)S(1)} %convolution_subtract_fusion.7), custom_call_target="Cholesky" | custom-call | tf_op jit(solution)/shard_map/jit(cholesky)/cholesky | solution.py:40
  325.0 19.7 %custom-call.24 = f32[2,128,128]{1,2,0:T(8,128)S(1)} custom-call(f32[2,128,128]{2,1,0:T(8,128)S(1)} %get-tuple-element.38), custom_call_target="InvertDiagBlocksLowerTriangular" | custom-call | tf_op jit(solution)/shard_map/jit(_solve_triangular)/triangular_solve | solution.py:41
  348.4 16.5 %collective-permute-done.3 = f32[768,256]{0,1:T(8,128)} collective-permute-done((f32[768,256]{0,1:T(8,128)S(1)}, f32[768,256]{0,1:T(8,128)}, u32[]{:S(2)}, u32[]{:S(2)}) %collective-permute-start.3) | collective-permute-done | bytes 786464 | tf_op jit(solution)/shard_map/ppermute | solution.py:15
  372.8 11.7 %cholesky.358 = f32[128,128]{1,0:T(8,128)S(1)} custom-call(f32[128,128]{1,0:T(8,128)S(1)} %cholesky.431), custom_call_target="Cholesky" | custom-call | tf_op jit(solution)/shard_map/jit(cholesky)/cholesky | solution.py:40
  396.7 11.9 %cholesky.375 = f32[128,128]{1,0:T(8,128)S(1)} custom-call(f32[128,128]{1,0:T(8,128)S(1)} %convolution_subtract_fusion.6), custom_call_target="Cholesky" | custom-call | tf_op jit(solution)/shard_map/jit(cholesky)/cholesky | solution.py:40
  417.7 20.5 %custom-call.26 = f32[2,128,128]{1,2,0:T(8,128)S(1)} custom-call(f32[2,128,128]{2,1,0:T(8,128)} %copy-done.7), custom_call_target="InvertDiagBlocksLowerTriangular" | custom-call | tf_op jit(solution)/shard_map/jit(_solve_triangular)/triangular_solve | solution.py:41
  449.2 29.7 %collective-permute-done.4 = f32[768,256]{0,1:T(8,128)} collective-permute-done((f32[768,256]{0,1:T(8,128)}, f32[768,256]{0,1:T(8,128)}, u32[]{:S(2)}, u32[]{:S(2)}) %collective-permute-start.4) | collective-permute-done | bytes 786464 | tf_op jit(solution)/shard_map/ppermute | solution.py:15
  484.2 11.7 %cholesky.392 = f32[128,128]{1,0:T(8,128)S(1)} custom-call(f32[128,128]{1,0:T(8,128)S(1)} %cholesky.434), custom_call_target="Cholesky" | custom-call | tf_op jit(solution)/shard_map/jit(cholesky)/cholesky | solution.py:40
  506.3 11.9 %cholesky.409 = f32[128,128]{1,0:T(8,128)S(1)} custom-call(f32[128,128]{1,0:T(8,128)S(1)} %convolution_subtract_fusion.5), custom_call_target="Cholesky" | custom-call | tf_op jit(solution)/shard_map/jit(cholesky)/cholesky | solution.py:40
  525.1 19.7 %custom-call.28 = f32[2,128,128]{1,2,0:T(8,128)S(1)} custom-call(f32[2,128,128]{2,1,0:T(8,128)S(1)} %get-tuple-element.40), custom_call_target="InvertDiagBlocksLowerTriangular" | custom-call | tf_op jit(solution)/shard_map/jit(_solve_triangular)/triangular_solve | solution.py:41
  (208 shorter events, 154.5 us)
Async XLA Ops:
  9.2 33.1 %all-to-all-start = ((bf16[8,256,256]{1,2,0:T(8,128)(2,1)}), bf16[8,256,256]{1,2,0:T(8,128)(2,1)S(1)}, u32[]{:S(2)}, u32[]{:S(2)}) async-start(bf16[8,256,256]{1,2,0:T(8,128)(2,1)} %stack.12), calls=%async_computation | async-start | bytes 2097152 | tf_op jit(solution)/shard_map/all_to_all | solution.py:83
  16.5 59.4 %all-reduce.3.cloned.1.call-start = ((), (), s32[]{:S(2)}) async-start(), calls=%async_computation.3 | async-start | bytes 1048576 | tf_op jit(solution)/shard_map/psum | solution.py:9
  43.4 60.6 %reduce-scatter.2.cloned.1.call-start = ((), (), s32[]{:S(2)}) async-start(), calls=%async_computation.2 | async-start | bytes 1310720 | tf_op jit(solution)/shard_map/reduce_scatter | solution.py:97
  43.6 5.8 %copy-start.6 = (f32[256,256]{1,0:T(8,128)S(1)}, f32[256,256]{1,0:T(8,128)}, u32[]{:S(2)}) copy-start(f32[256,256]{1,0:T(8,128)} %param.10) | copy-start | bytes 786436
  105.0 2.4 collective-permute-start
  173.3 19.7 %collective-permute-start.1 = (f32[768,256]{0,1:T(8,128)S(1)}, f32[768,256]{0,1:T(8,128)S(1)}, u32[]{:S(2)}, u32[]{:S(2)}) collective-permute-start(f32[768,256]{0,1:T(8,128)S(1)} %pad_maximum_fusion.2), channel_id=1, source_target_pairs={{0,2},{1,3},{2,0},{3,1},{4,6},{5,7},{6,4},{7,5},{8,10},{9,11},{10,... | collective-permute-start | bytes 2359304 | tf_op jit(solution)/shard_map/ppermute | solution.py:15
  258.8 18.9 %collective-permute-start.2 = (f32[768,256]{0,1:T(8,128)S(1)}, f32[768,256]{0,1:T(8,128)}, u32[]{:S(2)}, u32[]{:S(2)}) collective-permute-start(f32[768,256]{0,1:T(8,128)S(1)} %pad_maximum_fusion.3), channel_id=1, source_target_pairs={{0,4},{4,0},{8,12},{12,8},{16,20},{20,16},{24,28},{28,24},{1,5},{5... | collective-permute-start | bytes 2359304 | tf_op jit(solution)/shard_map/ppermute | solution.py:15
  346.9 18.0 %collective-permute-start.3 = (f32[768,256]{0,1:T(8,128)S(1)}, f32[768,256]{0,1:T(8,128)}, u32[]{:S(2)}, u32[]{:S(2)}) collective-permute-start(f32[768,256]{0,1:T(8,128)S(1)} %pad_maximum_fusion.4), channel_id=1, source_target_pairs={{0,8},{4,12},{8,0},{12,4},{16,24},{20,28},{24,16},{28,20},{1,9},{5... | collective-permute-start | bytes 2359304 | tf_op jit(solution)/shard_map/ppermute | solution.py:15
  372.7 11.8 %copy-start.5 = (f32[256,256]{1,0:T(8,128)}, f32[256,256]{1,0:T(8,128)S(1)}, u32[]{:S(2)}) copy-start(f32[256,256]{1,0:T(8,128)S(1)} %fusion.58) | copy-start | bytes 786436
  408.6 2.7 copy-start.1
  416.4 0.7 copy-start.7
  417.0 0.7 copy-start
  443.8 35.1 %collective-permute-start.4 = (f32[768,256]{0,1:T(8,128)}, f32[768,256]{0,1:T(8,128)}, u32[]{:S(2)}, u32[]{:S(2)}) collective-permute-start(f32[768,256]{0,1:T(8,128)} %pad_maximum_fusion.5), channel_id=1, source_target_pairs={{0,16},{4,20},{8,24},{12,28},{16,0},{20,4},{24,8},{28,12},{1,17},{... | collective-permute-start | bytes 2359304 | tf_op jit(solution)/shard_map/ppermute | solution.py:15
  483.2 63.1 %copy-start.2 = (f32[1,256,256]{2,1,0:T(8,128)S(1)}, f32[1,256,256]{2,1,0:T(8,128)}, u32[]{:S(2)}) copy-start(f32[1,256,256]{2,1,0:T(8,128)} %fusion.41) | copy-start | bytes 786436
  483.2 63.1 %copy-start.3 = (f32[1,256,256]{2,1,0:T(8,128)S(1)}, f32[1,256,256]{2,1,0:T(8,128)}, u32[]{:S(2)}) copy-start(f32[1,256,256]{2,1,0:T(8,128)} %fusion.37) | copy-start | bytes 786436
  483.2 63.1 %copy-start.4 = (f32[1,256,256]{2,1,0:T(8,128)S(1)}, f32[1,256,256]{2,1,0:T(8,128)}, u32[]{:S(2)}) copy-start(f32[1,256,256]{2,1,0:T(8,128)} %fusion.33) | copy-start | bytes 786436
Sparse Core Ops, SparseCore 0:
  43.5 32.4 all-reduce.2
  79.1 24.8 reduce-scatter.1
